TPU v7x, 32 devices: a whole 2x2x4 slice. The times are simulated.
32 devices in a mesh: ctx: 8 (over z, x), chan: 4 (over y, core).
Axes of the slice: x: 2, y: 2, z: 4, core: 2. Of those that a mesh axis runs over, the one named last changes fastest.
Arguments:
- query_in: bfloat16 [4096, 1024], P('chan', 'ctx'), may hold values from -6 to 6
- key_in: bfloat16 [4096, 1024], P('chan', 'ctx'), may hold values from -6 to 6
- value_in: bfloat16 [4096, 1024], P('chan', 'ctx'), may hold values from -6 to 6
- short_kernel: float32 [3, 3, 4096], P(None, None, 'chan'), may hold values from -3.5 to 3.5
- filter_in: float32 [64, 64], replicated, may hold values from -0.75 to 0.75
- filter_out: float32 [64, 4096], P(None, 'chan'), may hold values from -0.75 to 0.75
- filter_decay: float32 [4096], P('chan'), may hold values from 0.5 to 40
- skip_gain: float32 [4096], P('chan'), may hold values from -3 to 3
- grad_out: bfloat16 [4096, 1024], P('chan', 'ctx'), may hold values from -6 to 6
Outputs:
- output: bfloat16 [4096, 1024], P('chan', 'ctx')
- grad_query: bfloat16 [4096, 1024], P('chan', 'ctx')
- grad_key: bfloat16 [4096, 1024], P('chan', 'ctx')
- grad_value: bfloat16 [4096, 1024], P('chan', 'ctx')
- grad_short: float32 [3, 3, 4096], P(None, None, 'chan')
- grad_filter_in: float32 [64, 64], replicated
- grad_filter_out: float32 [64, 4096], P(None, 'chan')
- grad_decay: float32 [4096], P('chan')
- grad_skip: float32 [4096], P('chan')
All inputs are finite; a program needn't handle non-finite values.
Results may differ from a plain program's by a relative error of at most 0.0006.
Values may be sent and summed in bfloat16 or wider, within the bound.
No kernel may reach another device: no remote copies, remote signals or barrier semaphores. Data moves between devices by JAX's collectives and lax.ppermute only.
A program may use at most 128 MiB of HBM per device.

v0:
```python
import math
import jax
import jax.numpy as jnp
from jax import lax
from jax.sharding import PartitionSpec as P

PRECISE = lax.Precision.HIGHEST


def shifted(value, axis, by):
    peers = lax.axis_size(axis)
    pairs = [(i, i + by) for i in range(peers) if 0 <= i + by < peers]
    return lax.ppermute(value, axis, pairs)


def position_features(position, sequence, feature_rows):
    bands = jnp.arange(feature_rows // 2, dtype=jnp.int32)
    factor = 4 * (bands + 1) * (bands + 1)
    phase = position[None, :] * factor[:, None] % sequence
    angles = 2.0 * math.pi / sequence * phase.astype(jnp.float32)
    return jnp.concatenate([jnp.cos(angles), jnp.sin(angles)], axis=0)


def angle_tables(left_index, right_index, modulus):
    phase = left_index[:, None] * right_index[None, :] % modulus
    angles = 2.0 * math.pi / modulus * phase.astype(jnp.float32)
    return (jnp.cos(angles), jnp.sin(angles))


def contract(form, left, right):
    return jnp.einsum(form, left, right, precision=PRECISE)


def times_forward(real_part, imag_part, cosine, sine):
    return (real_part * cosine + imag_part * sine, imag_part * cosine - real_part * sine)


def times_inverse(real_part, imag_part, cosine, sine):
    return (real_part * cosine - imag_part * sine, imag_part * cosine + real_part * sine)


def complex_times(first_real, first_imag, second_real, second_imag):
    return (
        first_real * second_real - first_imag * second_imag,
        first_real * second_imag + first_imag * second_real,
    )


def local_forward(real_part, imag_part):
    length = real_part.shape[-1]
    inner = 64
    outer = length // inner
    leading = real_part.shape[:-1]
    real_part = real_part.reshape(leading + (outer, inner))
    imag_part = imag_part.reshape(leading + (outer, inner))
    outer_index = jnp.arange(outer, dtype=jnp.int32)
    inner_index = jnp.arange(inner, dtype=jnp.int32)
    cos_outer, sin_outer = angle_tables(outer_index, outer_index, outer)
    first_real = contract("cb,...ba->...ca", cos_outer, real_part) + contract(
        "cb,...ba->...ca", sin_outer, imag_part
    )
    first_imag = contract("cb,...ba->...ca", cos_outer, imag_part) - contract(
        "cb,...ba->...ca", sin_outer, real_part
    )
    cos_middle, sin_middle = angle_tables(outer_index, inner_index, length)
    first_real, first_imag = times_forward(first_real, first_imag, cos_middle, sin_middle)
    cos_inner, sin_inner = angle_tables(inner_index, inner_index, inner)
    final_real = contract("...ca,da->...cd", first_real, cos_inner) + contract(
        "...ca,da->...cd", first_imag, sin_inner
    )
    final_imag = contract("...ca,da->...cd", first_imag, cos_inner) - contract(
        "...ca,da->...cd", first_real, sin_inner
    )
    return (final_real, final_imag)


def local_inverse(real_part, imag_part):
    outer = real_part.shape[-2]
    inner = real_part.shape[-1]
    length = outer * inner
    leading = real_part.shape[:-2]
    outer_index = jnp.arange(outer, dtype=jnp.int32)
    inner_index = jnp.arange(inner, dtype=jnp.int32)
    cos_inner, sin_inner = angle_tables(inner_index, inner_index, inner)
    first_real = contract("...cd,ad->...ca", real_part, cos_inner) - contract(
        "...cd,ad->...ca", imag_part, sin_inner
    )
    first_imag = contract("...cd,ad->...ca", imag_part, cos_inner) + contract(
        "...cd,ad->...ca", real_part, sin_inner
    )
    cos_middle, sin_middle = angle_tables(outer_index, inner_index, length)
    first_real, first_imag = times_inverse(first_real, first_imag, cos_middle, sin_middle)
    cos_outer, sin_outer = angle_tables(outer_index, outer_index, outer)
    final_real = contract("bc,...ca->...ba", cos_outer, first_real) - contract(
        "bc,...ca->...ba", sin_outer, first_imag
    )
    final_imag = contract("bc,...ca->...ba", cos_outer, first_imag) + contract(
        "bc,...ca->...ba", sin_outer, first_real
    )
    return (final_real.reshape(leading + (length,)), final_imag.reshape(leading + (length,)))


def held_frequencies(device):
    return 2 * device + jnp.arange(2, dtype=jnp.int32)


def forward_spectrum(signals):
    shards = lax.axis_size("ctx")
    device = lax.axis_index("ctx")
    signal_count, channels, length = signals.shape
    padded = 2 * shards * length
    columns = lax.all_to_all(
        signals.reshape((1, signal_count, channels, length)),
        "ctx",
        split_axis=3,
        concat_axis=0,
        tiled=True,
    )
    shard_index = jnp.arange(shards, dtype=jnp.int32)
    freq_index = jnp.arange(2 * shards, dtype=jnp.int32)
    cos_table, sin_table = angle_tables(freq_index, shard_index, 2 * shards)
    rows_real = contract("qp,pmgb->qmgb", cos_table, columns)
    rows_imag = -contract("qp,pmgb->qmgb", sin_table, columns)
    arrived = lax.all_to_all(
        jnp.stack([rows_real, rows_imag]), "ctx", split_axis=1, concat_axis=4, tiled=True
    )
    spec_real = arrived[0]
    spec_imag = arrived[1]
    freqs = held_frequencies(device)
    cosine, sine = angle_tables(freqs, jnp.arange(length, dtype=jnp.int32), padded)
    spec_real, spec_imag = times_forward(
        spec_real, spec_imag, cosine[:, None, None, :], sine[:, None, None, :]
    )
    return local_forward(spec_real, spec_imag)


def inverse_columns(spec_real, spec_imag):
    shards = lax.axis_size("ctx")
    device = lax.axis_index("ctx")
    real_part, imag_part = local_inverse(spec_real, spec_imag)
    length = real_part.shape[-1]
    padded = 2 * shards * length
    freqs = held_frequencies(device)
    cosine, sine = angle_tables(freqs, jnp.arange(length, dtype=jnp.int32), padded)
    real_part, imag_part = times_inverse(
        real_part, imag_part, cosine[:, None, None, :], sine[:, None, None, :]
    )
    shard_index = jnp.arange(shards, dtype=jnp.int32)
    arrived = lax.all_to_all(
        jnp.stack([real_part, imag_part]), "ctx", split_axis=4, concat_axis=1, tiled=True
    )
    cos_table, sin_table = angle_tables(
        shard_index, jnp.arange(2 * shards, dtype=jnp.int32), 2 * shards
    )
    columns = contract("pq,qmgb->pmgb", cos_table, arrived[0]) - contract(
        "pq,qmgb->pmgb", sin_table, arrived[1]
    )
    return columns * (1.0 / padded)


def to_tokens(columns):
    arrived = lax.all_to_all(columns, "ctx", split_axis=0, concat_axis=3, tiled=True)
    return arrived[0]


def body(
    query_in,
    key_in,
    value_in,
    short_kernel,
    filter_in,
    filter_out,
    filter_decay,
    skip_gain,
    grad_out,
):
    shards = lax.axis_size("ctx")
    device = lax.axis_index("ctx")
    length = query_in.shape[1]
    sequence = shards * length
    scale = sequence ** (-0.5)
    inputs = jnp.stack([query_in, key_in, value_in])
    rim = shifted(inputs[:, :, -2:], "ctx", 1)
    values = inputs.astype(jnp.float32)
    rim_values = rim.astype(jnp.float32)
    before_one = jnp.concatenate([rim_values[..., 1:], values[..., :-1]], axis=-1)
    before_two = jnp.concatenate([rim_values, values[..., :-2]], axis=-1)
    kernel = short_kernel[:, :, :, None]
    shorted = kernel[:, 0] * values + kernel[:, 1] * before_one + kernel[:, 2] * before_two
    query_short = shorted[0]
    key_short = shorted[1]
    value_short = shorted[2]
    gate = key_short * value_short
    position = device * length + jnp.arange(length, dtype=jnp.int32)
    fraction = position.astype(jnp.float32) / sequence
    basis = position_features(position, sequence, filter_in.shape[0])
    preact = jnp.dot(filter_in.T, basis, precision=PRECISE)
    hidden = jnp.sin(preact)
    window = jnp.exp(-filter_decay[:, None] * fraction[None, :])
    taps = window * jnp.dot(filter_out.T, hidden, precision=PRECISE) * scale
    spec_real, spec_imag = forward_spectrum(jnp.stack([gate, taps]))
    gate_real, gate_imag = (spec_real[:, 0], spec_imag[:, 0])
    taps_real, taps_imag = (spec_real[:, 1], spec_imag[:, 1])
    prod_real, prod_imag = complex_times(gate_real, gate_imag, taps_real, taps_imag)
    conv = to_tokens(inverse_columns(prod_real[:, None], prod_imag[:, None]))[0]
    mixed = conv + skip_gain[:, None] * gate
    output = (query_short * mixed).astype(jnp.bfloat16)
    upstream = grad_out.astype(jnp.float32)
    grad_mixed = upstream * query_short
    grad_query_short = upstream * mixed
    upper_real, upper_imag = forward_spectrum(grad_mixed[None])
    upper_real = upper_real[:, 0]
    upper_imag = upper_imag[:, 0]
    along_real, along_imag = complex_times(taps_real, -taps_imag, upper_real, upper_imag)
    cross_real, cross_imag = complex_times(gate_real, -gate_imag, upper_real, upper_imag)
    backward = to_tokens(
        inverse_columns(
            jnp.stack([along_real, cross_real], axis=1), jnp.stack([along_imag, cross_imag], axis=1)
        )
    )
    grad_gate = backward[0] + skip_gain[:, None] * grad_mixed
    grad_taps = backward[1]
    grads = jnp.stack([grad_query_short, grad_gate * value_short, grad_gate * key_short])
    after = shifted(grads[..., :2], "ctx", -1)
    next_one = jnp.concatenate([grads[..., 1:], after[..., :1]], axis=-1)
    next_two = jnp.concatenate([grads[..., 2:], after], axis=-1)
    grad_inputs = (kernel[:, 0] * grads + kernel[:, 1] * next_one + kernel[:, 2] * next_two).astype(
        jnp.bfloat16
    )
    short_terms = jnp.stack(
        [
            jnp.sum(grads * values, axis=-1),
            jnp.sum(grads * before_one, axis=-1),
            jnp.sum(grads * before_two, axis=-1),
        ],
        axis=1,
    )
    weighted = grad_taps * window * scale
    out_terms = jnp.dot(hidden, weighted.T, precision=PRECISE)
    grad_hidden = jnp.dot(filter_out, weighted, precision=PRECISE)
    in_terms = jnp.dot(basis, (grad_hidden * jnp.cos(preact)).T, precision=PRECISE)
    decay_terms = jnp.sum(grad_taps * taps * -fraction[None, :], axis=1)
    skip_terms = jnp.sum(grad_mixed * gate, axis=1)
    short_sum, out_sum, decay_sum, skip_sum = lax.psum(
        (short_terms, out_terms, decay_terms, skip_terms), "ctx"
    )
    in_sum = lax.psum(in_terms, ("ctx", "chan"))
    return (
        output,
        grad_inputs[0],
        grad_inputs[1],
        grad_inputs[2],
        short_sum * scale,
        in_sum * scale,
        out_sum * scale,
        decay_sum * scale,
        skip_sum * scale,
    )


def solution(mesh):
    placed = (
        P("chan", "ctx"),
        P("chan", "ctx"),
        P("chan", "ctx"),
        P(None, None, "chan"),
        P(),
        P(None, "chan"),
        P("chan"),
        P("chan"),
        P("chan", "ctx"),
    )
    return jax.shard_map(
        body,
        mesh=mesh,
        in_specs=placed,
        out_specs=(
            P("chan", "ctx"),
            P("chan", "ctx"),
            P("chan", "ctx"),
            P("chan", "ctx"),
            P(None, None, "chan"),
            P(),
            P(None, "chan"),
            P("chan"),
            P("chan"),
        ),
        check_vma=False,
    )
```

profile of v0, /device:TPU:0, one launch (start us, length us, event | category | flops | bytes accessed | tf_op | source)
XLA Modules:
  0.0 651.2 jit_solution(13803028707653949594)
XLA Ops:
  11.0 4.8 collective-permute-start
  20.5 6.6 %all-to-all-start.4 = ((f32[1,1,1024,128]{2,1,0,3:T(1,128)}), f32[1,1,1024,128]{2,1,0,3:T(1,128)}, u32[]{:S(2)}, u32[]{:S(2)}) async-start(f32[1,1,1024,128]{2,1,0,3:T(1,128)} %copy.246), calls=%async_computation.4 | async-start | bytes 1048576 | tf_op jit(solution)/shard_map/all_to_all | solution.py:112
  32.8 7.8 %all-to-all-done.4 = f32[1,1,1024,128]{2,1,0,3:T(1,128)} async-done(((f32[1,1,1024,128]{2,1,0,3:T(1,128)}), f32[1,1,1024,128]{2,1,0,3:T(1,128)}, u32[]{:S(2)}, u32[]{:S(2)}) %all-to-all-start.4) | async-done | bytes 524320 | tf_op jit(solution)/shard_map/all_to_all | solution.py:112
  40.6 4.2 all-to-all-start
  51.2 18.4 %all-to-all-done = f32[1,2,1024,128]{2,1,0,3:T(2,128)} async-done(((f32[1,2,1024,128]{2,1,0,3:T(2,128)}), f32[1,2,1024,128]{2,1,0,3:T(2,128)}, u32[]{:S(2)}, u32[]{:S(2)}) %all-to-all-start) | async-done | bytes 1048608 | tf_op jit(solution)/shard_map/all_to_all | solution.py:112
  69.6 4.8 all-to-all-start.5
  74.4 3.4 negate_bitcast_fusion
  77.9 3.4 convolution_bitcast_fusion
  81.9 4.4 copy.220
  86.3 35.7 %all-to-all-done.5 = f32[2,16,1,1024,16]{3,4,2,0,1:T(8,128)} async-done(((f32[2,16,1,1024,16]{3,4,2,0,1:T(8,128)}), f32[2,16,1,1024,16]{3,4,2,0,1:T(8,128)}, u32[]{:S(2)}, u32[]{:S(2)}) %all-to-all-start.5) | async-done | bytes 2097184 | tf_op jit(solution)/shard_map/all_to_all | solution.py:124
  122.0 4.7 all-to-all-start.1
  132.9 4.1 fusion.61
  136.9 4.3 fusion.35
  141.3 4.1 fusion.65
  145.3 5.7 subtract_bitcast_fusion.1
  157.5 61.7 %all-to-all-done.1 = f32[2,16,2,1024,16]{3,4,2,0,1:T(8,128)} async-done(((f32[2,16,2,1024,16]{3,4,2,0,1:T(8,128)}), f32[2,16,2,1024,16]{3,4,2,0,1:T(8,128)}, u32[]{:S(2)}, u32[]{:S(2)}) %all-to-all-start.1) | async-done | bytes 4194336 | tf_op jit(solution)/shard_map/all_to_all | solution.py:124
  224.1 7.9 %fusion.26 = f32[2,2,1024,64,2]{2,4,3,1,0:T(2,128)S(1)} fusion(f32[2,2,1024,2,64]{2,4,3,1,0:T(8,128)S(1)} %get-tuple-element.68), kind=kOutput, calls=%fused_computation.48 | convolution fusion | flops 12582968 | bytes 4194304 | tf_op jit(solution)/shard_map/cb,...ba->...ca/dot_general | solution.py:31
  232.0 8.3 %fusion.22 = f32[2,2,1024,64,2]{2,4,3,1,0:T(2,128)S(1)} fusion(f32[2,2,1024,2,64]{2,4,3,1,0:T(8,128)S(1)} %get-tuple-element.69), kind=kOutput, calls=%fused_computation.44 | convolution fusion | flops 12582968 | bytes 4194304 | tf_op jit(solution)/shard_map/cb,...ba->...ca/dot_general | solution.py:31
  240.3 8.2 %convolution_add_fusion = f32[2,2,1024,64,2]{2,4,3,1,0:T(2,128)S(1)} fusion(f32[2,2,1024,64,2]{2,4,3,1,0:T(2,128)S(1)} %fusion.26, f32[2,2,1024,2,64]{2,4,3,1,0:T(8,128)S(1)} %get-tuple-element.69), kind=kOutput, calls=%fused_computation.42 | convolution fusion | flops 13107256 | bytes 6291456 | tf_op jit(solution)/shard_map/cb,...ba->...ca/dot_general | solution.py:31
  248.6 11.2 %fusion.2 = (f32[2,2,1024,2,64]{2,3,4,1,0:T(2,128)S(1)}, f32[2,2,1024,2,64]{2,3,4,1,0:T(2,128)S(1)}) fusion(f32[2,2,1024,64,2]{2,4,3,1,0:T(2,128)S(1)} %convolution_add_fusion, f32[2,64]{0,1:T(8,128)S(1)} %copy-done.21, f32[2,64]{0,1:T(8,128)S(1)} %copy-done.23, f32[2,2,1024,64,2]{2,4,3,1,0:T(2,128)S(1)} %fusion.22, ...), kind=kOutput, calls=%fused_computation.14 | convolution fusion | flops 16252984 | bytes 10486784 | tf_op jit(solution)/shard_map/cb,...ba->...ca/dot_general | solution.py:31
  265.4 3.1 fusion.16
  268.6 3.1 fusion.19
  271.7 3.9 multiply_subtract_fusion.3
  284.9 9.6 %multiply_subtract_fusion = (f32[2,2,1024,2,64]{2,3,4,1,0:T(2,128)S(1)}, f32[2,2,1024,2,64]{2,3,4,1,0:T(2,128)S(1)}) fusion(f32[2,64]{0,1:T(8,128)S(1)} %copy-done.21, f32[2,64]{0,1:T(8,128)S(1)} %copy-done.23, f32[2,2,1024,2,64]{2,4,3,1,0:T(8,128)S(1)} %fusion.13, f32[2,2,1024,2,64]{2,4,3,1,0:T(8,128)S(1)} %fusion.15, ...), kind=kLoop, calls=%fused_computation.23 | loop fusion | flops 4194304 | bytes 12583936 | tf_op jit(solution)/shard_map/sub | solution.py:39
  294.5 7.5 %fusion.190 = f32[2,2,1024,64,2]{2,4,3,1,0:T(2,128)S(1)} fusion(f32[2,2,1024,2,64]{2,3,4,1,0:T(2,128)S(1)} %get-tuple-element.60), kind=kOutput, calls=%fused_computation.283 | convolution fusion | flops 12582968 | bytes 4194304 | tf_op jit(solution)/shard_map/bc,...ca->...ba/dot_general | solution.py:31
  302.0 7.5 %fusion.188 = f32[2,2,1024,64,2]{2,4,3,1,0:T(2,128)S(1)} fusion(f32[2,2,1024,2,64]{2,3,4,1,0:T(2,128)S(1)} %get-tuple-element.61), kind=kOutput, calls=%fused_computation.281 | convolution fusion | flops 12582968 | bytes 4194304 | tf_op jit(solution)/shard_map/bc,...ca->...ba/dot_general | solution.py:31
  309.6 8.4 %subtract_bitcast_fusion = f32[2,2,1024,2,64]{2,3,4,1,0:T(2,128)S(1)} fusion(f32[2,2,1024,64,2]{2,4,3,1,0:T(2,128)S(1)} %fusion.190, f32[2,2,1024,2,64]{2,3,4,1,0:T(2,128)S(1)} %get-tuple-element.61), kind=kOutput, calls=%fused_computation.21 | convolution fusion | flops 13107256 | bytes 6291456 | tf_op jit(solution)/shard_map/bc,...ca->...ba/dot_general | solution.py:31
  317.9 8.0 %add_bitcast_fusion = f32[2,2,1024,2,64]{2,3,4,1,0:T(2,128)S(1)} fusion(f32[2,2,1024,64,2]{2,4,3,1,0:T(2,128)S(1)} %fusion.188, f32[2,2,1024,2,64]{2,3,4,1,0:T(2,128)S(1)} %get-tuple-element.60), kind=kOutput, calls=%fused_computation.20 | convolution fusion | flops 13107256 | bytes 6291456 | tf_op jit(solution)/shard_map/bc,...ca->...ba/dot_general | solution.py:31
  328.8 5.2 copy.268
  334.0 5.0 all-to-all-start.6
  345.8 4.1 fusion.67
  349.8 4.3 fusion.37
  354.5 4.1 fusion.71
  358.5 4.4 fusion.38
  366.8 64.8 %all-to-all-done.6 = f32[2,2,2,1024,128]{3,2,1,0,4:T(2,128)} async-done(((f32[2,2,2,1024,128]{3,2,1,0,4:T(2,128)}), f32[2,2,2,1024,128]{3,2,1,0,4:T(2,128)}, u32[]{:S(2)}, u32[]{:S(2)}) %all-to-all-start.6) | async-done | bytes 4194336 | tf_op jit(solution)/shard_map/all_to_all | solution.py:149
  431.5 4.4 all-to-all-start.2
  435.9 4.6 copy.269
  445.3 3.7 squeeze.65
  449.1 4.6 copy.270
  453.7 3.7 squeeze.64
  462.9 20.8 %all-to-all-done.2 = f32[2,2,1,1024,128]{3,1,2,0,4:T(2,128)} async-done(((f32[2,2,1,1024,128]{3,1,2,0,4:T(2,128)}), f32[2,2,1,1024,128]{3,1,2,0,4:T(2,128)}, u32[]{:S(2)}, u32[]{:S(2)}) %all-to-all-start.2) | async-done | bytes 2097184 | tf_op jit(solution)/shard_map/all_to_all | solution.py:149
  483.7 4.5 all-to-all-start.7
  496.9 3.0 copy.242
  506.5 7.3 %all-to-all-done.7 = f32[8,2,1024,16]{2,3,1,0:T(8,128)} async-done(((f32[8,2,1024,16]{2,3,1,0:T(8,128)}), f32[8,2,1024,16]{2,3,1,0:T(8,128)}, u32[]{:S(2)}, u32[]{:S(2)}) %all-to-all-start.7) | async-done | bytes 1048608 | tf_op jit(solution)/shard_map/all_to_all | solution.py:162
  513.8 4.1 all-to-all-start.3
  523.4 40.9 %psum.36 = f32[64,64]{1,0:T(8,128)S(1)} all-reduce(f32[64,64]{1,0:T(8,128)} %fusion.105), channel_id=1, replica_groups=mesh['ctx'=8,'chan'=4] {'ctx','chan'}, use_global_device_ids=true, to_apply=%region_4.5 | all-reduce | flops 4096 | bytes 32768 | tf_op jit(solution)/shard_map/psum | solution.py:247
  574.1 37.3 %all-reduce = (f32[3,3,1024]{2,0,1:T(4,128)S(1)}, f32[1024]{0:T(1024)S(1)}, f32[1024]{0:T(1024)S(1)}) all-reduce(f32[3,3,1024]{2,0,1:T(4,128)S(1)} %pad_maximum_fusion.14, f32[1024]{0:T(1024)S(1)} %get-tuple-element.106, f32[1024]{0:T(1024)S(1)} %get-tuple-element.96), channel_id=1, replica_groups=mesh['ctx'=8,'chan'=4] {'ctx'}, use_global_device_ids=true, to_apply=%region_3.4 | all-reduce | flops 11264 | bytes 90112 | tf_op jit(solution)/shard_map/psum | solution.py:244
  621.0 21.3 %all-reduce.3.cloned.1.call-done = f32[64,1024]{1,0:T(8,128)} async-done(((f32[64,1024]{1,0:T(8,128)}), f32[64,1024]{1,0:T(8,128)}) %all-reduce.3.cloned.1.call-update) | async-done | bytes 262160 | tf_op jit(solution)/shard_map/psum | solution.py:244
  (188 shorter events, 118.8 us)
Async XLA Ops:
  7.2 22.2 %copy-start = (f32[64,1024]{1,0:T(8,128)S(1)}, f32[64,1024]{1,0:T(8,128)}, u32[]{:S(2)}) copy-start(f32[64,1024]{1,0:T(8,128)} %param.14) | copy-start | bytes 786436
  8.3 2.6 copy-start.10
  8.3 7.5 %copy-start.27 = (f32[3,3,1024]{2,1,0:T(4,128)S(1)}, f32[3,3,1024]{2,1,0:T(4,128)}, u32[]{:S(2)}) copy-start(f32[3,3,1024]{2,1,0:T(4,128)} %param.12) | copy-start | bytes 110596
  8.3 7.7 %copy-start.36 = (f32[1024]{0:T(1024)S(1)}, f32[1024]{0:T(1024)}, u32[]{:S(2)}) copy-start(f32[1024]{0:T(1024)} %param.15) | copy-start | bytes 12292
  8.4 7.8 %copy-start.19 = (bf16[1024,128]{1,0:T(8,128)(2,1)S(1)}, bf16[1024,128]{1,0:T(8,128)(2,1)}, u32[]{:S(2)}) copy-start(bf16[1024,128]{1,0:T(8,128)(2,1)} %param.17) | copy-start | bytes 786436
  9.6 7.4 %copy-start.11 = (bf16[1024,128]{0,1:T(8,128)(2,1)}, bf16[1024,128]{0,1:T(8,128)(2,1)S(1)}, u32[]{:S(2)}) copy-start(bf16[1024,128]{0,1:T(8,128)(2,1)S(1)} %copy.215) | copy-start | bytes 786436
  10.8 6.5 copy-start.12
  11.0 6.2 collective-permute-start
  17.3 1.8 copy-start.25
  17.3 1.7 copy-start.18
  20.5 20.0 %all-to-all-start.4 = ((f32[1,1,1024,128]{2,1,0,3:T(1,128)}), f32[1,1,1024,128]{2,1,0,3:T(1,128)}, u32[]{:S(2)}, u32[]{:S(2)}) async-start(f32[1,1,1024,128]{2,1,0,3:T(1,128)} %copy.246), calls=%async_computation.4 | async-start | bytes 1048576 | tf_op jit(solution)/shard_map/all_to_all | solution.py:112
  27.7 1.7 copy-start.37
  30.1 0.8 copy-start.8
  40.6 29.0 %all-to-all-start = ((f32[1,2,1024,128]{2,1,0,3:T(2,128)}), f32[1,2,1024,128]{2,1,0,3:T(2,128)}, u32[]{:S(2)}, u32[]{:S(2)}) async-start(f32[1,2,1024,128]{2,1,0,3:T(2,128)} %copy.217), calls=%async_computation | async-start | bytes 2097152 | tf_op jit(solution)/shard_map/all_to_all | solution.py:112
  69.6 52.4 %all-to-all-start.5 = ((f32[2,16,1,1024,16]{3,4,2,0,1:T(8,128)}), f32[2,16,1,1024,16]{3,4,2,0,1:T(8,128)}, u32[]{:S(2)}, u32[]{:S(2)}) async-start(f32[2,16,1,1024,16]{3,4,2,0,1:T(8,128)} %copy.248), calls=%async_computation.5 | async-start | bytes 4194304 | tf_op jit(solution)/shard_map/all_to_all | solution.py:124
  122.0 97.3 %all-to-all-start.1 = ((f32[2,16,2,1024,16]{3,4,2,0,1:T(8,128)}), f32[2,16,2,1024,16]{3,4,2,0,1:T(8,128)}, u32[]{:S(2)}, u32[]{:S(2)}) async-start(f32[2,16,2,1024,16]{3,4,2,0,1:T(8,128)} %copy.220), calls=%async_computation.1 | async-start | bytes 8388608 | tf_op jit(solution)/shard_map/all_to_all | solution.py:124
  127.4 2.1 copy-start.30
  130.3 2.2 copy-start.28
  141.2 4.1 copy-start.20
  141.2 4.1 copy-start.22
  151.1 4.0 copy-start.15
  222.6 0.7 copy-start.29
  240.3 8.3 %copy-start.21 = (f32[2,64]{0,1:T(8,128)S(1)}, f32[2,64]{0,1:T(8,128)}, u32[]{:S(2)}) copy-start(f32[2,64]{0,1:T(8,128)} %copy.229) | copy-start | bytes 1540
  240.3 8.3 %copy-start.23 = (f32[2,64]{0,1:T(8,128)S(1)}, f32[2,64]{0,1:T(8,128)}, u32[]{:S(2)}) copy-start(f32[2,64]{0,1:T(8,128)} %copy.226) | copy-start | bytes 1540
  268.5 3.1 copy-start.14
  268.6 3.1 copy-start.16
  268.6 3.1 copy-start.17
  326.5 0.7 copy-start.33
  334.0 97.5 %all-to-all-start.6 = ((f32[2,2,2,1024,128]{3,2,1,0,4:T(2,128)}), f32[2,2,2,1024,128]{3,2,1,0,4:T(2,128)}, u32[]{:S(2)}, u32[]{:S(2)}) async-start(f32[2,2,2,1024,128]{3,2,1,0,4:T(2,128)} %copy.268), calls=%async_computation.6 | async-start | bytes 8388608 | tf_op jit(solution)/shard_map/all_to_all | solution.py:149
  339.0 2.6 copy-start.1
  339.0 3.8 copy-start.2
  342.9 1.3 copy-start.31
  342.9 1.3 copy-start.32
  358.5 4.7 copy-start.35
  431.5 52.2 %all-to-all-start.2 = ((f32[2,2,1,1024,128]{3,1,2,0,4:T(2,128)}), f32[2,2,1,1024,128]{3,1,2,0,4:T(2,128)}, u32[]{:S(2)}, u32[]{:S(2)}) async-start(f32[2,2,1,1024,128]{3,1,2,0,4:T(2,128)} %copy.240), calls=%async_computation.2 | async-start | bytes 4194304 | tf_op jit(solution)/shard_map/all_to_all | solution.py:149
  457.3 2.9 copy-start.3
  483.7 30.1 %all-to-all-start.7 = ((f32[8,2,1024,16]{2,3,1,0:T(8,128)}), f32[8,2,1024,16]{2,3,1,0:T(8,128)}, u32[]{:S(2)}, u32[]{:S(2)}) async-start(f32[8,2,1024,16]{2,3,1,0:T(8,128)} %copy.272), calls=%async_computation.7 | async-start | bytes 2097152 | tf_op jit(solution)/shard_map/all_to_all | solution.py:162
  502.8 2.0 copy-start.13
  513.8 53.3 %all-to-all-start.3 = ((f32[8,1,1024,16]{2,3,1,0:T(8,128)}), f32[8,1,1024,16]{2,3,1,0:T(8,128)}, u32[]{:S(2)}, u32[]{:S(2)}) async-start(f32[8,1,1024,16]{2,3,1,0:T(8,128)} %copy.244), calls=%async_computation.3 | async-start | bytes 1048576 | tf_op jit(solution)/shard_map/all_to_all | solution.py:162
  517.9 124.3 %all-reduce.3.cloned.1.call-start = ((), (), s32[]{:S(2)}) async-start(), calls=%async_computation.8 | async-start | bytes 524288 | tf_op jit(solution)/shard_map/psum | solution.py:244
  518.0 2.2 copy-start.9
  518.0 3.9 copy-start.24
  521.1 0.8 copy-start.7
  567.0 4.7 copy-start.26
  612.0 5.7 collective-permute-start.1
  614.1 3.7 copy-start.4
  614.1 3.7 copy-start.5
  614.1 3.7 copy-start.6
  (1 other events, 0.7 us)
Sparse Core Ops, SparseCore 0:
  571.8 70.4 all-reduce.2
where the time goes:
time: 659 us; the launch traced here: 651 us
  waiting for transfers between devices  241 us (37%)
  matrix products  162 us (25%)
  local copies, waits for them, and re-layouts  82.3 us (12%)
  blocking collectives  78.2 us (12%)
  starting transfers between devices  44.5 us (7%)
  other arithmetic  28.1 us (4%)
  between operations  15.7 us (2%)
    dot_general x40, matrix products, contract(): return jnp.einsum(form, left, right, precision=PRECISE)  156 us
    all_to_all x2, waiting for transfers between devices, forward_spectrum(): lax.all_to_all(jnp.stack([rows_real, rows_imag]), 'ctx', split_axis=1, co...  97.4 us
    all_to_all x2, waiting for transfers between devices, inverse_columns(): lax.all_to_all(jnp.stack([real_part, imag_part]), 'ctx', split_axis=4, co...  85.6 us
    psum x1, blocking collectives, body(): in_sum = lax.psum(in_terms, ('ctx', 'chan'))  40.9 us
    psum x1, blocking collectives, body(): lax.psum((short_terms, out_terms, decay_terms, skip_terms), 'ctx')  37.3 us
    all_to_all x2, waiting for transfers between devices, forward_spectrum(): lax.all_to_all(signals.reshape((1, signal_count, channels, length)), 'ctx...  26.2 us
    psum x1, waiting for transfers between devices, body(): lax.psum((short_terms, out_terms, decay_terms, skip_terms), 'ctx')  21.3 us
  transfers between devices with their start and end apart: 11, of which 10 were waited for; matrix products, arithmetic and copies ran while one was open for 22% of the time, Pallas kernels for 0%

commit v1 on v0

--- a/solution.py
+++ b/solution.py
@@ -3,6 +3,7 @@
 import jax.numpy as jnp
 from jax import lax
 from jax.sharding import PartitionSpec as P
+from jax.lax import psum
 
 PRECISE = lax.Precision.HIGHEST
 
@@ -244,7 +245,9 @@
     short_sum, out_sum, decay_sum, skip_sum = lax.psum(
         (short_terms, out_terms, decay_terms, skip_terms), "ctx"
     )
-    in_sum = lax.psum(in_terms, ("ctx", "chan"))
+    in_sum = in_terms
+    for q in ("chan", "ctx"):
+        in_sum = psum(in_sum, axis_name=q)
     return (
         output,
         grad_inputs[0],

time: 659 us -> 631 us (0.958)
  blocking collectives: 78.2 us -> 49.7 us
    psum x1, blocking collectives: 40.9 us -> 11.2 us  [body(): in_sum = psum(in_sum, axis_name=q)]
  transfers between devices with their start and end apart: 11 -> 11, of which waited for: 10 -> 10; matrix products, arithmetic and copies ran while one was open for 22% -> 23% of each run, Pallas kernels for 0% -> 0%
where the time goes in v1:
time: 631 us; the launch traced here: 623 us
  waiting for transfers between devices  240 us (38%)
  matrix products  162 us (26%)
  local copies, waits for them, and re-layouts  82.3 us (13%)
  blocking collectives  49.7 us (8%)
  starting transfers between devices  44.5 us (7%)
  other arithmetic  28.1 us (4%)
  between operations  15.7 us (2%)
    dot_general x40, matrix products, contract(): return jnp.einsum(form, left, right, precision=PRECISE)  156 us
    all_to_all x2, waiting for transfers between devices, forward_spectrum(): lax.all_to_all(jnp.stack([rows_real, rows_imag]), 'ctx', split_axis=1, co...  97.4 us
    all_to_all x2, waiting for transfers between devices, inverse_columns(): lax.all_to_all(jnp.stack([real_part, imag_part]), 'ctx', split_axis=4, co...  85.6 us
    psum x1, blocking collectives, body(): lax.psum((short_terms, out_terms, decay_terms, skip_terms), 'ctx')  38.6 us
    all_to_all x2, waiting for transfers between devices, forward_spectrum(): lax.all_to_all(signals.reshape((1, signal_count, channels, length)), 'ctx...  26.2 us
    psum x1, waiting for transfers between devices, body(): lax.psum((short_terms, out_terms, decay_terms, skip_terms), 'ctx')  21.1 us
    unnamed x88, local copies, waits for them, and re-layouts  12.7 us
  transfers between devices with their start and end apart: 11, of which 10 were waited for; matrix products, arithmetic and copies ran while one was open for 23% of the time, Pallas kernels for 0%

profile of v1, /device:TPU:0, one launch (start us, length us, event | category | flops | bytes accessed | tf_op | source)
XLA Modules:
  0.0 622.5 jit_solution(553772671685644068)
XLA Ops:
  11.0 4.8 collective-permute-start
  20.5 6.6 %all-to-all-start.4 = ((f32[1,1,1024,128]{2,1,0,3:T(1,128)}), f32[1,1,1024,128]{2,1,0,3:T(1,128)}, u32[]{:S(2)}, u32[]{:S(2)}) async-start(f32[1,1,1024,128]{2,1,0,3:T(1,128)} %copy.246), calls=%async_computation.4 | async-start | bytes 1048576 | tf_op jit(solution)/shard_map/all_to_all | solution.py:113
  32.8 7.8 %all-to-all-done.4 = f32[1,1,1024,128]{2,1,0,3:T(1,128)} async-done(((f32[1,1,1024,128]{2,1,0,3:T(1,128)}), f32[1,1,1024,128]{2,1,0,3:T(1,128)}, u32[]{:S(2)}, u32[]{:S(2)}) %all-to-all-start.4) | async-done | bytes 524320 | tf_op jit(solution)/shard_map/all_to_all | solution.py:113
  40.6 4.2 all-to-all-start
  51.2 18.4 %all-to-all-done = f32[1,2,1024,128]{2,1,0,3:T(2,128)} async-done(((f32[1,2,1024,128]{2,1,0,3:T(2,128)}), f32[1,2,1024,128]{2,1,0,3:T(2,128)}, u32[]{:S(2)}, u32[]{:S(2)}) %all-to-all-start) | async-done | bytes 1048608 | tf_op jit(solution)/shard_map/all_to_all | solution.py:113
  69.6 4.8 all-to-all-start.5
  74.4 3.4 negate_bitcast_fusion
  77.9 3.4 convolution_bitcast_fusion
  81.9 4.4 copy.220
  86.3 35.7 %all-to-all-done.5 = f32[2,16,1,1024,16]{3,4,2,0,1:T(8,128)} async-done(((f32[2,16,1,1024,16]{3,4,2,0,1:T(8,128)}), f32[2,16,1,1024,16]{3,4,2,0,1:T(8,128)}, u32[]{:S(2)}, u32[]{:S(2)}) %all-to-all-start.5) | async-done | bytes 2097184 | tf_op jit(solution)/shard_map/all_to_all | solution.py:125
  122.0 4.7 all-to-all-start.1
  132.9 4.1 fusion.61
  136.9 4.3 fusion.35
  141.3 4.1 fusion.65
  145.3 5.7 subtract_bitcast_fusion.1
  157.5 61.7 %all-to-all-done.1 = f32[2,16,2,1024,16]{3,4,2,0,1:T(8,128)} async-done(((f32[2,16,2,1024,16]{3,4,2,0,1:T(8,128)}), f32[2,16,2,1024,16]{3,4,2,0,1:T(8,128)}, u32[]{:S(2)}, u32[]{:S(2)}) %all-to-all-start.1) | async-done | bytes 4194336 | tf_op jit(solution)/shard_map/all_to_all | solution.py:125
  224.1 7.9 %fusion.26 = f32[2,2,1024,64,2]{2,4,3,1,0:T(2,128)S(1)} fusion(f32[2,2,1024,2,64]{2,4,3,1,0:T(8,128)S(1)} %get-tuple-element.69), kind=kOutput, calls=%fused_computation.48 | convolution fusion | flops 12582968 | bytes 4194304 | tf_op jit(solution)/shard_map/cb,...ba->...ca/dot_general | solution.py:32
  232.0 8.3 %fusion.22 = f32[2,2,1024,64,2]{2,4,3,1,0:T(2,128)S(1)} fusion(f32[2,2,1024,2,64]{2,4,3,1,0:T(8,128)S(1)} %get-tuple-element.70), kind=kOutput, calls=%fused_computation.44 | convolution fusion | flops 12582968 | bytes 4194304 | tf_op jit(solution)/shard_map/cb,...ba->...ca/dot_general | solution.py:32
  240.3 8.2 %convolution_add_fusion = f32[2,2,1024,64,2]{2,4,3,1,0:T(2,128)S(1)} fusion(f32[2,2,1024,64,2]{2,4,3,1,0:T(2,128)S(1)} %fusion.26, f32[2,2,1024,2,64]{2,4,3,1,0:T(8,128)S(1)} %get-tuple-element.70), kind=kOutput, calls=%fused_computation.42 | convolution fusion | flops 13107256 | bytes 6291456 | tf_op jit(solution)/shard_map/cb,...ba->...ca/dot_general | solution.py:32
  248.6 11.2 %fusion.2 = (f32[2,2,1024,2,64]{2,3,4,1,0:T(2,128)S(1)}, f32[2,2,1024,2,64]{2,3,4,1,0:T(2,128)S(1)}) fusion(f32[2,2,1024,64,2]{2,4,3,1,0:T(2,128)S(1)} %convolution_add_fusion, f32[2,64]{0,1:T(8,128)S(1)} %copy-done.21, f32[2,64]{0,1:T(8,128)S(1)} %copy-done.23, f32[2,2,1024,64,2]{2,4,3,1,0:T(2,128)S(1)} %fusion.22, ...), kind=kOutput, calls=%fused_computation.14 | convolution fusion | flops 16252984 | bytes 10486784 | tf_op jit(solution)/shard_map/cb,...ba->...ca/dot_general | solution.py:32
  265.4 3.1 fusion.16
  268.6 3.1 fusion.19
  271.7 3.9 multiply_subtract_fusion.3
  284.9 9.6 %multiply_subtract_fusion = (f32[2,2,1024,2,64]{2,3,4,1,0:T(2,128)S(1)}, f32[2,2,1024,2,64]{2,3,4,1,0:T(2,128)S(1)}) fusion(f32[2,64]{0,1:T(8,128)S(1)} %copy-done.21, f32[2,64]{0,1:T(8,128)S(1)} %copy-done.23, f32[2,2,1024,2,64]{2,4,3,1,0:T(8,128)S(1)} %fusion.13, f32[2,2,1024,2,64]{2,4,3,1,0:T(8,128)S(1)} %fusion.15, ...), kind=kLoop, calls=%fused_computation.23 | loop fusion | flops 4194304 | bytes 12583936 | tf_op jit(solution)/shard_map/sub | solution.py:40
  294.5 7.5 %fusion.190 = f32[2,2,1024,64,2]{2,4,3,1,0:T(2,128)S(1)} fusion(f32[2,2,1024,2,64]{2,3,4,1,0:T(2,128)S(1)} %get-tuple-element.61), kind=kOutput, calls=%fused_computation.283 | convolution fusion | flops 12582968 | bytes 4194304 | tf_op jit(solution)/shard_map/bc,...ca->...ba/dot_general | solution.py:32
  302.0 7.5 %fusion.188 = f32[2,2,1024,64,2]{2,4,3,1,0:T(2,128)S(1)} fusion(f32[2,2,1024,2,64]{2,3,4,1,0:T(2,128)S(1)} %get-tuple-element.62), kind=kOutput, calls=%fused_computation.281 | convolution fusion | flops 12582968 | bytes 4194304 | tf_op jit(solution)/shard_map/bc,...ca->...ba/dot_general | solution.py:32
  309.6 8.4 %subtract_bitcast_fusion = f32[2,2,1024,2,64]{2,3,4,1,0:T(2,128)S(1)} fusion(f32[2,2,1024,64,2]{2,4,3,1,0:T(2,128)S(1)} %fusion.190, f32[2,2,1024,2,64]{2,3,4,1,0:T(2,128)S(1)} %get-tuple-element.62), kind=kOutput, calls=%fused_computation.21 | convolution fusion | flops 13107256 | bytes 6291456 | tf_op jit(solution)/shard_map/bc,...ca->...ba/dot_general | solution.py:32
  317.9 8.0 %add_bitcast_fusion = f32[2,2,1024,2,64]{2,3,4,1,0:T(2,128)S(1)} fusion(f32[2,2,1024,64,2]{2,4,3,1,0:T(2,128)S(1)} %fusion.188, f32[2,2,1024,2,64]{2,3,4,1,0:T(2,128)S(1)} %get-tuple-element.61), kind=kOutput, calls=%fused_computation.20 | convolution fusion | flops 13107256 | bytes 6291456 | tf_op jit(solution)/shard_map/bc,...ca->...ba/dot_general | solution.py:32
  328.8 5.2 copy.268
  334.0 5.0 all-to-all-start.6
  345.8 4.1 fusion.67
  349.8 4.3 fusion.37
  354.5 4.1 fusion.71
  358.5 4.4 fusion.38
  366.8 64.8 %all-to-all-done.6 = f32[2,2,2,1024,128]{3,2,1,0,4:T(2,128)} async-done(((f32[2,2,2,1024,128]{3,2,1,0,4:T(2,128)}), f32[2,2,2,1024,128]{3,2,1,0,4:T(2,128)}, u32[]{:S(2)}, u32[]{:S(2)}) %all-to-all-start.6) | async-done | bytes 4194336 | tf_op jit(solution)/shard_map/all_to_all | solution.py:150
  431.5 4.4 all-to-all-start.2
  435.9 4.6 copy.269
  445.3 3.7 squeeze.65
  449.1 4.6 copy.270
  453.7 3.7 squeeze.64
  462.9 20.8 %all-to-all-done.2 = f32[2,2,1,1024,128]{3,1,2,0,4:T(2,128)} async-done(((f32[2,2,1,1024,128]{3,1,2,0,4:T(2,128)}), f32[2,2,1,1024,128]{3,1,2,0,4:T(2,128)}, u32[]{:S(2)}, u32[]{:S(2)}) %all-to-all-start.2) | async-done | bytes 2097184 | tf_op jit(solution)/shard_map/all_to_all | solution.py:150
  483.7 4.5 all-to-all-start.7
  496.9 3.0 copy.242
  506.5 7.3 %all-to-all-done.7 = f32[8,2,1024,16]{2,3,1,0:T(8,128)} async-done(((f32[8,2,1024,16]{2,3,1,0:T(8,128)}), f32[8,2,1024,16]{2,3,1,0:T(8,128)}, u32[]{:S(2)}, u32[]{:S(2)}) %all-to-all-start.7) | async-done | bytes 1048608 | tf_op jit(solution)/shard_map/all_to_all | solution.py:163
  513.8 4.1 all-to-all-start.3
  523.4 11.2 %psum.43 = f32[64,64]{1,0:T(8,128)S(1)} all-reduce(f32[64,64]{1,0:T(8,128)} %fusion.105), channel_id=1, replica_groups=mesh['ctx'=8,'chan'=4] {'chan'}, use_global_device_ids=true, to_apply=%region_4.5 | all-reduce | flops 4096 | bytes 32768 | tf_op jit(solution)/shard_map/psum | solution.py:250
  543.8 38.6 %all-reduce = (f32[3,3,1024]{2,0,1:T(4,128)S(1)}, f32[64,64]{1,0:T(8,128)S(1)}, f32[1024]{0:T(1024)S(1)}, f32[1024]{0:T(1024)S(1)}) all-reduce(f32[3,3,1024]{2,0,1:T(4,128)S(1)} %pad_maximum_fusion.14, f32[64,64]{1,0:T(8,128)S(1)} %psum.43, f32[1024]{0:T(1024)S(1)} %get-tuple-element.106, ...), channel_id=1, replica_groups=mesh['ctx'=8,'chan'=4] {'ctx'}, use_global_device_ids=true, to_apply=%region_3.4 | all-reduce | flops 15360 | bytes 122880 | tf_op jit(solution)/shard_map/psum | solution.py:245
  592.5 21.1 %all-reduce.3.cloned.1.call-done = f32[64,1024]{1,0:T(8,128)} async-done(((f32[64,1024]{1,0:T(8,128)}), f32[64,1024]{1,0:T(8,128)}) %all-reduce.3.cloned.1.call-update) | async-done | bytes 262160 | tf_op jit(solution)/shard_map/psum | solution.py:245
  (188 shorter events, 118.8 us)
Async XLA Ops:
  7.2 22.2 %copy-start = (f32[64,1024]{1,0:T(8,128)S(1)}, f32[64,1024]{1,0:T(8,128)}, u32[]{:S(2)}) copy-start(f32[64,1024]{1,0:T(8,128)} %param.14) | copy-start | bytes 786436
  8.3 2.6 copy-start.10
  8.3 7.5 %copy-start.27 = (f32[3,3,1024]{2,1,0:T(4,128)S(1)}, f32[3,3,1024]{2,1,0:T(4,128)}, u32[]{:S(2)}) copy-start(f32[3,3,1024]{2,1,0:T(4,128)} %param.12) | copy-start | bytes 110596
  8.3 7.7 %copy-start.36 = (f32[1024]{0:T(1024)S(1)}, f32[1024]{0:T(1024)}, u32[]{:S(2)}) copy-start(f32[1024]{0:T(1024)} %param.15) | copy-start | bytes 12292
  8.4 7.8 %copy-start.19 = (bf16[1024,128]{1,0:T(8,128)(2,1)S(1)}, bf16[1024,128]{1,0:T(8,128)(2,1)}, u32[]{:S(2)}) copy-start(bf16[1024,128]{1,0:T(8,128)(2,1)} %param.17) | copy-start | bytes 786436
  9.6 7.4 %copy-start.11 = (bf16[1024,128]{0,1:T(8,128)(2,1)}, bf16[1024,128]{0,1:T(8,128)(2,1)S(1)}, u32[]{:S(2)}) copy-start(bf16[1024,128]{0,1:T(8,128)(2,1)S(1)} %copy.215) | copy-start | bytes 786436
  10.8 6.5 %copy-start.12 = (bf16[1024,128]{0,1:T(8,128)(2,1)}, bf16[1024,128]{0,1:T(8,128)(2,1)S(1)}, u32[]{:S(2)}) copy-start(bf16[1024,128]{0,1:T(8,128)(2,1)S(1)} %copy.216) | copy-start | bytes 786436
  11.0 6.2 %collective-permute-start = (bf16[3,1024,2]{1,2,0:T(2,128)(2,1)S(1)}, bf16[3,1024,2]{1,2,0:T(2,128)(2,1)S(1)}, u32[]{:S(2)}, u32[]{:S(2)}) collective-permute-start(bf16[3,1024,2]{1,2,0:T(2,128)(2,1)S(1)} %slice.139), channel_id=1, source_target_pairs={{0,4},{4,8},{8,12},{12,16},{16,20},{20,24},{24,28},{1,5},{5,9},{9,... | collective-permute-start | bytes 36872 | tf_op jit(solution)/shard_map/ppermute | solution.py:14
  17.3 1.8 copy-start.25
  17.3 1.7 copy-start.18
  20.5 20.0 %all-to-all-start.4 = ((f32[1,1,1024,128]{2,1,0,3:T(1,128)}), f32[1,1,1024,128]{2,1,0,3:T(1,128)}, u32[]{:S(2)}, u32[]{:S(2)}) async-start(f32[1,1,1024,128]{2,1,0,3:T(1,128)} %copy.246), calls=%async_computation.4 | async-start | bytes 1048576 | tf_op jit(solution)/shard_map/all_to_all | solution.py:113
  27.7 1.7 copy-start.37
  30.1 0.8 copy-start.8
  40.6 29.0 %all-to-all-start = ((f32[1,2,1024,128]{2,1,0,3:T(2,128)}), f32[1,2,1024,128]{2,1,0,3:T(2,128)}, u32[]{:S(2)}, u32[]{:S(2)}) async-start(f32[1,2,1024,128]{2,1,0,3:T(2,128)} %copy.217), calls=%async_computation | async-start | bytes 2097152 | tf_op jit(solution)/shard_map/all_to_all | solution.py:113
  69.6 52.4 %all-to-all-start.5 = ((f32[2,16,1,1024,16]{3,4,2,0,1:T(8,128)}), f32[2,16,1,1024,16]{3,4,2,0,1:T(8,128)}, u32[]{:S(2)}, u32[]{:S(2)}) async-start(f32[2,16,1,1024,16]{3,4,2,0,1:T(8,128)} %copy.248), calls=%async_computation.5 | async-start | bytes 4194304 | tf_op jit(solution)/shard_map/all_to_all | solution.py:125
  122.0 97.3 %all-to-all-start.1 = ((f32[2,16,2,1024,16]{3,4,2,0,1:T(8,128)}), f32[2,16,2,1024,16]{3,4,2,0,1:T(8,128)}, u32[]{:S(2)}, u32[]{:S(2)}) async-start(f32[2,16,2,1024,16]{3,4,2,0,1:T(8,128)} %copy.220), calls=%async_computation.1 | async-start | bytes 8388608 | tf_op jit(solution)/shard_map/all_to_all | solution.py:125
  127.4 2.1 copy-start.30
  130.3 2.2 copy-start.28
  141.2 4.1 copy-start.20
  141.2 4.1 copy-start.22
  151.1 4.0 copy-start.15
  222.6 0.7 copy-start.29
  240.3 8.3 %copy-start.21 = (f32[2,64]{0,1:T(8,128)S(1)}, f32[2,64]{0,1:T(8,128)}, u32[]{:S(2)}) copy-start(f32[2,64]{0,1:T(8,128)} %copy.229) | copy-start | bytes 1540
  240.3 8.3 %copy-start.23 = (f32[2,64]{0,1:T(8,128)S(1)}, f32[2,64]{0,1:T(8,128)}, u32[]{:S(2)}) copy-start(f32[2,64]{0,1:T(8,128)} %copy.226) | copy-start | bytes 1540
  268.5 3.1 copy-start.14
  268.6 3.1 copy-start.16
  268.6 3.1 copy-start.17
  326.5 0.7 copy-start.33
  334.0 97.5 %all-to-all-start.6 = ((f32[2,2,2,1024,128]{3,2,1,0,4:T(2,128)}), f32[2,2,2,1024,128]{3,2,1,0,4:T(2,128)}, u32[]{:S(2)}, u32[]{:S(2)}) async-start(f32[2,2,2,1024,128]{3,2,1,0,4:T(2,128)} %copy.268), calls=%async_computation.6 | async-start | bytes 8388608 | tf_op jit(solution)/shard_map/all_to_all | solution.py:150
  339.0 2.6 copy-start.1
  339.0 3.8 copy-start.2
  342.9 1.3 copy-start.31
  342.9 1.3 copy-start.32
  358.5 4.7 copy-start.35
  431.5 52.2 %all-to-all-start.2 = ((f32[2,2,1,1024,128]{3,1,2,0,4:T(2,128)}), f32[2,2,1,1024,128]{3,1,2,0,4:T(2,128)}, u32[]{:S(2)}, u32[]{:S(2)}) async-start(f32[2,2,1,1024,128]{3,1,2,0,4:T(2,128)} %copy.240), calls=%async_computation.2 | async-start | bytes 4194304 | tf_op jit(solution)/shard_map/all_to_all | solution.py:150
  457.3 2.9 copy-start.3
  483.7 30.1 %all-to-all-start.7 = ((f32[8,2,1024,16]{2,3,1,0:T(8,128)}), f32[8,2,1024,16]{2,3,1,0:T(8,128)}, u32[]{:S(2)}, u32[]{:S(2)}) async-start(f32[8,2,1024,16]{2,3,1,0:T(8,128)} %copy.272), calls=%async_computation.7 | async-start | bytes 2097152 | tf_op jit(solution)/shard_map/all_to_all | solution.py:163
  502.8 2.0 copy-start.13
  513.8 22.9 %all-to-all-start.3 = ((f32[8,1,1024,16]{2,3,1,0:T(8,128)}), f32[8,1,1024,16]{2,3,1,0:T(8,128)}, u32[]{:S(2)}, u32[]{:S(2)}) async-start(f32[8,1,1024,16]{2,3,1,0:T(8,128)} %copy.244), calls=%async_computation.3 | async-start | bytes 1048576 | tf_op jit(solution)/shard_map/all_to_all | solution.py:163
  517.9 95.7 %all-reduce.3.cloned.1.call-start = ((), (), s32[]{:S(2)}) async-start(), calls=%async_computation.8 | async-start | bytes 524288 | tf_op jit(solution)/shard_map/psum | solution.py:245
  518.0 2.2 copy-start.9
  518.0 3.9 copy-start.24
  521.1 0.8 copy-start.7
  536.7 4.7 copy-start.26
  583.6 5.7 collective-permute-start.1
  585.6 3.7 copy-start.4
  585.6 3.7 copy-start.5
  585.7 3.7 copy-start.6
  (1 other events, 0.7 us)
Sparse Core Ops, SparseCore 0:
  541.5 72.0 all-reduce.2
